TPU v7x, 32 devices: a whole 2x2x4 slice. The times are simulated.
32 devices in a mesh: row: 4 (over x, core), col: 8 (over z, y).
Axes of the slice: x: 2, y: 2, z: 4, core: 2. Of those that a mesh axis runs over, the one named last changes fastest.
Arguments:
- signatures: bfloat16 [2048, 49152], P('row', 'col'), as said below
- trailing: float32 [2048, 1024], P('row', 'col'), may hold values from -6 to 6
- ridge: float32 [1], replicated, may hold values from 0.5 to 2
- panel_index: int32 [1], replicated, may hold values from 1 to 3
Outputs:
- factor: float32 [2048, 256], P(('row', 'col'))
- updated: float32 [2048, 1024], P('row', 'col')
Inputs may be any that keep to these rules, and one draw needn't show every extreme that they name: `signatures`: every diagonal block of the Gram matrix plus the ridge is positive definite.
All inputs are finite; a program needn't handle non-finite values.
Results may differ from a plain program's by a relative error of at most 0.0003.
Values may be sent and summed in bfloat16 or wider, within the bound.
A program may use at most 64 MiB of HBM per device.

v0:
```python
import jax
import jax.numpy as jnp
from jax import lax
from jax.sharding import PartitionSpec as P

PANEL = 256


def spread(block, axis, owner):
    block = jnp.where(lax.axis_index(axis) == owner, block, jnp.zeros_like(block))
    return lax.psum(block, axis)


def add_ridge(block, first_row, panel_start, ridge):
    row_ids = first_row + lax.broadcasted_iota(jnp.int32, block.shape, 0)
    col_ids = panel_start + lax.broadcasted_iota(jnp.int32, block.shape, 1)
    return block + jnp.where(row_ids == col_ids, ridge[0], jnp.zeros((), block.dtype))


def mask_above(block, first_row, panel_start):
    row_ids = first_row + lax.broadcasted_iota(jnp.int32, block.shape, 0)
    return jnp.where(row_ids >= panel_start, block, jnp.zeros((), block.dtype))


def solve_rows(lower, panel_rows):
    return jax.scipy.linalg.solve_triangular(lower, panel_rows.T, lower=True).T


def local(signatures, trailing, ridge, panel_index):
    rows_dev = signatures.shape[0]
    tile_cols = trailing.shape[1]
    col_count = lax.axis_size("col")
    row_share = rows_dev // col_count
    row_pos = lax.axis_index("row")
    col_pos = lax.axis_index("col")
    panel_start = panel_index[0] * PANEL
    row_owner = panel_start // rows_dev
    local_offset = panel_start % rows_dev
    own_paths = lax.dynamic_slice_in_dim(signatures, local_offset, PANEL, 0)
    panel_paths = spread(own_paths, "row", row_owner)
    mine_rows = lax.psum_scatter(
        lax.dot_general(
            signatures, panel_paths, (((1,), (1,)), ((), ())), preferred_element_type=jnp.float32
        ),
        "col",
        scatter_dimension=0,
        tiled=True,
    )
    mine_rows = add_ridge(mine_rows, row_pos * rows_dev + col_pos * row_share, panel_start, ridge)
    own_block = lax.dot_general(
        panel_paths, panel_paths, (((1,), (1,)), ((), ())), preferred_element_type=jnp.float32
    )
    diagonal = lax.psum(own_block, "col")
    diagonal = add_ridge(diagonal, panel_start, panel_start, ridge)
    lower = jnp.linalg.cholesky(diagonal)
    factor_mine = solve_rows(lower, mine_rows)
    factor_mine = mask_above(factor_mine, row_pos * rows_dev + col_pos * row_share, panel_start)
    factor_block = lax.all_gather(factor_mine, "col", axis=0, tiled=True)
    window_start = panel_start + PANEL + col_pos * tile_cols
    window_owner = window_start // rows_dev
    window_cut = lax.dynamic_slice_in_dim(factor_block, window_start % rows_dev, tile_cols, 0)
    window_rows = spread(window_cut, "row", window_owner)
    updated = trailing - lax.dot_general(
        factor_block,
        window_rows,
        (((1,), (1,)), ((), ())),
        precision=lax.Precision.HIGHEST,
        preferred_element_type=jnp.float32,
    )
    return (factor_mine, updated)


def solution(mesh):
    placed = (P("row", "col"), P("row", "col"), P(), P())
    return jax.shard_map(
        local,
        mesh=mesh,
        in_specs=placed,
        out_specs=(P(("row", "col"), None), P("row", "col")),
        check_vma=False,
    )
```

profile of v0, /device:TPU:0, one launch (start us, length us, event | category | flops | bytes accessed | tf_op | source)
XLA Modules:
  0.0 299.6 jit_solution(7277814875881397498)
XLA Ops:
  7.2 0.0 all-reduce.5.cloned.1.call-start
  7.9 4.5 %dynamic-slice_select_fusion = bf16[256,6144]{1,0:T(8,128)(2,1)} fusion(bf16[512,6144]{1,0:T(8,128)(2,1)} %param.4, s32[]{:T(128)S(6)} %select_n.62, pred[]{:T(512)S(6)} %eq.15), kind=kLoop, calls=%fused_computation.2 | loop fusion | flops 1572864 | bytes 6291461 | tf_op jit(solution)/shard_map/jit(_where)/select_n | solution.py:10
  12.4 0.0 all-reduce.5.cloned.1.call-update
  12.5 0.0 all-reduce.7.cloned.1.call-start
  13.3 70.5 %all-reduce.5.cloned.1.call-done = bf16[256,6144]{1,0:T(8,128)(2,1)} async-done(((bf16[256,6144]{1,0:T(8,128)(2,1)}), bf16[256,6144]{1,0:T(8,128)(2,1)}) %all-reduce.5.cloned.1.call-update) | async-done | bytes 3145744 | tf_op jit(solution)/shard_map/psum | solution.py:11
  83.8 4.6 %fusion.10 = f32[256,256]{0,1:T(8,128)} fusion(bf16[256,6144]{1,0:T(8,128)(2,1)} %all-reduce.5.cloned.1.call-done), kind=kOutput, calls=%fused_computation.39 | convolution fusion | flops 805306368 | bytes 3407872 | tf_op jit(solution)/shard_map/dot_general | solution.py:50
  88.3 0.0 all-reduce.7.cloned.1.call-update
  88.3 0.0 reduce-scatter.4.cloned.1.call-start
  88.4 5.6 %convolution_bitcast_fusion = f32[512,256]{0,1:T(8,128)S(1)} fusion(bf16[256,6144]{1,0:T(8,128)(2,1)} %all-reduce.5.cloned.1.call-done, bf16[512,6144]{1,0:T(8,128)(2,1)} %param.4), kind=kOutput, calls=%fused_computation.3 | convolution fusion | flops 1610612736 | bytes 9961472 | tf_op jit(solution)/shard_map/dot_general | solution.py:42
  94.0 1.0 copy.19
  95.0 0.0 reduce-scatter.4.cloned.1.call-update
  95.0 0.2 all-reduce.9.cloned.1.call-start
  95.2 64.4 %all-reduce.7.cloned.1.call-done = f32[256,256]{0,1:T(8,128)} async-done(((f32[256,256]{0,1:T(8,128)}), f32[256,256]{0,1:T(8,128)}) %all-reduce.7.cloned.1.call-update) | async-done | bytes 262160 | tf_op jit(solution)/shard_map/psum | solution.py:53
  159.6 1.0 select_add_fusion
  160.7 0.1 copy.13
  160.8 1.1 fusion
  161.9 11.7 %cholesky.49 = f32[128,128]{1,0:T(8,128)S(1)} custom-call(f32[128,128]{1,0:T(8,128)S(1)} %cholesky.115), custom_call_target="Cholesky" | custom-call | tf_op jit(solution)/shard_map/jit(cholesky)/cholesky | solution.py:55
  173.7 9.8 %custom-call.15 = f32[1,128,128]{1,2,0:T(8,128)S(1)} custom-call(f32[1,128,128]{2,1,0:T(8,128)S(1)} %get-tuple-element.29), custom_call_target="InvertDiagBlocksLowerTriangular" | custom-call | tf_op jit(solution)/shard_map/jit(cholesky)/cholesky | solution.py:55
  183.5 0.0 copy-start.1
  183.5 0.2 fusion.5
  183.7 0.3 convolution_subtract_fusion.2
  184.0 11.7 %cholesky.103 = f32[128,128]{1,0:T(8,128)S(1)} custom-call(f32[128,128]{1,0:T(8,128)S(1)} %convolution_subtract_fusion.2), custom_call_target="Cholesky" | custom-call | tf_op jit(solution)/shard_map/jit(cholesky)/cholesky | solution.py:55
  195.7 0.1 copy.16
  195.8 0.1 copy.15
  195.9 0.1 copy.14
  196.0 0.6 compare_reduce_fusion
  198.1 0.1 triangular_solve.60
  198.1 4.4 %while.1 = (s32[]{:T(128)}, f32[256,256]{0,1:T(8,128)S(1)}, s32[2,2]{1,0:T(2,128)S(1)}, f32[2,128,128]{2,1,0:T(8,128)S(1)}, s32[]{:T(128)}) while((s32[]{:T(128)}, f32[256,256]{0,1:T(8,128)S(1)}, s32[2,2]{1,0:T(2,128)S(1)}, f32[2,128,128]{2,1,0:T(8,128)S(1)}, s32[]{:T(128)}) %tuple.27), condition=%wide.while_cond, body=%wide.while_body.sunk | while | flops 2 | bytes 393321 | solution.py:26
  198.3 0.6 fusion.22
  198.9 1.4 dynamic-slice.7
  200.3 0.1 copy.23
  200.4 0.6 fusion.22
  201.0 1.4 dynamic-slice.7
  202.4 0.1 copy.23
  202.5 19.7 %custom-call.16 = f32[2,128,128]{1,2,0:T(8,128)S(1)} custom-call(f32[2,128,128]{2,1,0:T(8,128)S(1)} %get-tuple-element.9), custom_call_target="InvertDiagBlocksLowerTriangular" | custom-call | tf_op jit(solution)/shard_map/jit(_solve_triangular)/triangular_solve | solution.py:26
  222.2 3.6 %reduce-scatter.4.cloned.1.call-done = f32[64,256]{1,0:T(8,128)} async-done(((f32[512,256]{1,0:T(8,128)}), f32[64,256]{1,0:T(8,128)}) %reduce-scatter.4.cloned.1.call-update) | async-done | bytes 65552
  225.8 0.9 copy.20
  226.7 0.1 add_bitcast_fusion
  226.8 0.3 fusion.3
  227.1 0.3 convolution_subtract_fusion.1
  227.4 0.3 fusion.2
  227.7 0.1 fusion.7
  227.8 0.0 copy-start
  227.8 31.4 %all_gather.3 = f32[512,256]{1,0:T(8,128)S(1)} all-gather(f32[64,256]{1,0:T(8,128)S(1)} %fusion.7), channel_id=1, replica_groups=mesh['row'=4,'col'=8] {'col'}, dimensions={0}, use_global_device_ids=true | all-gather | bytes 589824 | tf_op jit(solution)/shard_map/all_gather | solution.py:58
  259.2 0.7 dynamic-slice_select_fusion.1
  259.9 0.0 all-reduce.9.cloned.1.call-update
  259.9 30.9 %all-reduce.9.cloned.1.call-done = f32[128,256]{1,0:T(8,128)} async-done(((f32[128,256]{1,0:T(8,128)}), f32[128,256]{1,0:T(8,128)}) %all-reduce.9.cloned.1.call-update) | async-done | bytes 131088 | tf_op jit(solution)/shard_map/psum | solution.py:11
  290.8 0.0 copy-done.1
  290.9 2.2 convolution_subtract_fusion
  293.0 0.0 copy-done
  (16 shorter events, 0.2 us)
Async XLA Ops:
  7.2 76.6 %all-reduce.5.cloned.1.call-start = ((), (), s32[]{:S(2)}) async-start(), calls=%async_computation.1 | async-start | bytes 6291456 | tf_op jit(solution)/shard_map/psum | solution.py:11
  12.5 147.2 %all-reduce.7.cloned.1.call-start = ((), (), s32[]{:S(2)}) async-start(), calls=%async_computation.2 | async-start | bytes 524288 | tf_op jit(solution)/shard_map/psum | solution.py:53
  88.3 137.4 %reduce-scatter.4.cloned.1.call-start = ((), (), s32[]{:S(2)}) async-start(), calls=%async_computation.4 | async-start | bytes 589824
  95.0 195.9 %all-reduce.9.cloned.1.call-start = ((), (), s32[]{:S(2)}) async-start(), calls=%async_computation.3 | async-start | bytes 262144 | tf_op jit(solution)/shard_map/psum | solution.py:11
  183.5 107.4 %copy-start.1 = (f32[512,128]{1,0:T(8,128)S(1)}, f32[512,128]{1,0:T(8,128)}, u32[]{:S(2)}) copy-start(f32[512,128]{1,0:T(8,128)} %param.5) | copy-start | bytes 786436
  227.8 65.3 %copy-start = (f32[64,256]{1,0:T(8,128)}, f32[64,256]{1,0:T(8,128)S(1)}, u32[]{:S(2)}) copy-start(f32[64,256]{1,0:T(8,128)S(1)} %fusion.7) | copy-start | bytes 196612
Sparse Core Ops, SparseCore 0:
  12.6 71.1 all-reduce.4
  88.5 71.1 all-reduce.6
  163.0 62.7 reduce-scatter.3
  260.0 30.7 all-reduce.8
where the time goes:
time: 300 us
  waiting for transfers between devices  169 us (56%)
  other arithmetic  61.2 us (20%)
  blocking collectives  31.4 us (10%)
  between operations  16.7 us (6%)
  matrix products  13.6 us (5%)
  local copies, waits for them, and re-layouts  6.6 us (2%)
    psum x2, waiting for transfers between devices, spread(): return lax.psum(block, axis)  101 us
    psum x1, waiting for transfers between devices, local(): diagonal = lax.psum(own_block, 'col')  64.4 us
    another operation x6, other arithmetic, local(): lower = jnp.linalg.cholesky(diagonal)  34 us
    all_gather x1, blocking collectives, local(): factor_block = lax.all_gather(factor_mine, 'col', axis=0, tiled=True)  31.4 us
    another operation x3, other arithmetic, solve_rows(): return jax.scipy.linalg.solve_triangular(lower, panel_rows.T, lower=True).T  19.7 us
  transfers between devices with their start and end apart: 4, of which 4 were waited for; matrix products, arithmetic and copies ran while one was open for 23% of the time, Pallas kernels for 0%

commit v1 on v0

--- a/solution.py
+++ b/solution.py
@@ -55,7 +55,12 @@
     lower = jnp.linalg.cholesky(diagonal)
     factor_mine = solve_rows(lower, mine_rows)
     factor_mine = mask_above(factor_mine, row_pos * rows_dev + col_pos * row_share, panel_start)
-    factor_block = lax.all_gather(factor_mine, "col", axis=0, tiled=True)
+    ring = [factor_mine]
+    for hop in range(7):
+        ring.append(lax.ppermute(ring[-1], "col", [(dev, (dev + 1) % 8) for dev in range(8)]))
+    factor_block = jnp.roll(
+        jnp.concatenate(ring[::-1], axis=0), (lax.axis_index("col") + 1) * ring[0].shape[0], axis=0
+    )
     window_start = panel_start + PANEL + col_pos * tile_cols
     window_owner = window_start // rows_dev
     window_cut = lax.dynamic_slice_in_dim(factor_block, window_start % rows_dev, tile_cols, 0)

time: 300 us -> 316 us (1.053)
  waiting for transfers between devices: 169 us -> 215 us
  blocking collectives: 31.4 us -> 0 us
    ppermute x0 -> x7, waiting for transfers between devices: none -> 47.6 us  [local(): lax.ppermute(ring[-1], 'col', [(dev, (dev + 1) % 8) for dev in range(8)])]
    all_gather x1 -> x0, blocking collectives: 31.4 us -> none  [local(): factor_block = lax.all_gather(factor_mine, 'col', axis=0, tiled=True)]
  transfers between devices with their start and end apart: 4 -> 11, of which waited for: 4 -> 11; matrix products, arithmetic and copies ran while one was open for 23% -> 21% of each run, Pallas kernels for 0% -> 0%
where the time goes in v1:
time: 316 us; the launch traced here: 315 us
  waiting for transfers between devices  215 us (68%)
  other arithmetic  61.2 us (19%)
  between operations  16.8 us (5%)
  matrix products  13.6 us (4%)
  local copies, waits for them, and re-layouts  6.76 us (2%)
    psum x2, waiting for transfers between devices, spread(): return lax.psum(block, axis)  99.7 us
    psum x1, waiting for transfers between devices, local(): diagonal = lax.psum(own_block, 'col')  64.4 us
    ppermute x7, waiting for transfers between devices, local(): lax.ppermute(ring[-1], 'col', [(dev, (dev + 1) % 8) for dev in range(8)])  47.6 us
    another operation x6, other arithmetic, local(): lower = jnp.linalg.cholesky(diagonal)  34 us
    another operation x3, other arithmetic, solve_rows(): return jax.scipy.linalg.solve_triangular(lower, panel_rows.T, lower=True).T  19.7 us
  transfers between devices with their start and end apart: 11, of which 11 were waited for; matrix products, arithmetic and copies ran while one was open for 21% of the time, Pallas kernels for 0%

profile of v1, /device:TPU:0, one launch (start us, length us, event | category | flops | bytes accessed | tf_op | source)
XLA Modules:
  0.0 315.2 jit_solution(15775272627234800372)
XLA Ops:
  7.2 0.0 all-reduce.5.cloned.1.call-start
  7.9 4.5 %dynamic-slice_select_fusion = bf16[256,6144]{1,0:T(8,128)(2,1)} fusion(bf16[512,6144]{1,0:T(8,128)(2,1)} %param.4, s32[]{:T(128)S(6)} %select_n.78, pred[]{:T(512)S(6)} %eq.18), kind=kLoop, calls=%fused_computation.2 | loop fusion | flops 1572864 | bytes 6291461 | tf_op jit(solution)/shard_map/jit(_where)/select_n | solution.py:10
  12.4 0.0 all-reduce.5.cloned.1.call-update
  12.4 0.0 all-reduce.7.cloned.1.call-start
  13.2 70.5 %all-reduce.5.cloned.1.call-done = bf16[256,6144]{1,0:T(8,128)(2,1)} async-done(((bf16[256,6144]{1,0:T(8,128)(2,1)}), bf16[256,6144]{1,0:T(8,128)(2,1)}) %all-reduce.5.cloned.1.call-update) | async-done | bytes 3145744 | tf_op jit(solution)/shard_map/psum | solution.py:11
  83.7 4.6 %fusion.12 = f32[256,256]{0,1:T(8,128)} fusion(bf16[256,6144]{1,0:T(8,128)(2,1)} %all-reduce.5.cloned.1.call-done), kind=kOutput, calls=%fused_computation.57 | convolution fusion | flops 805306368 | bytes 3407872 | tf_op jit(solution)/shard_map/dot_general | solution.py:50
  88.3 0.0 all-reduce.7.cloned.1.call-update
  88.3 0.0 reduce-scatter.4.cloned.1.call-start
  88.4 5.6 %convolution_bitcast_fusion = f32[512,256]{0,1:T(8,128)S(1)} fusion(bf16[256,6144]{1,0:T(8,128)(2,1)} %all-reduce.5.cloned.1.call-done, bf16[512,6144]{1,0:T(8,128)(2,1)} %param.4), kind=kOutput, calls=%fused_computation.3 | convolution fusion | flops 1610612736 | bytes 9961472 | tf_op jit(solution)/shard_map/dot_general | solution.py:42
  94.0 1.0 copy.19
  94.9 0.0 reduce-scatter.4.cloned.1.call-update
  95.0 0.2 all-reduce.9.cloned.1.call-start
  95.2 64.4 %all-reduce.7.cloned.1.call-done = f32[256,256]{0,1:T(8,128)} async-done(((f32[256,256]{0,1:T(8,128)}), f32[256,256]{0,1:T(8,128)}) %all-reduce.7.cloned.1.call-update) | async-done | bytes 262160 | tf_op jit(solution)/shard_map/psum | solution.py:53
  159.6 1.0 select_add_fusion
  160.7 0.1 copy.13
  160.8 1.1 fusion.1
  161.9 11.7 %cholesky.49 = f32[128,128]{1,0:T(8,128)S(1)} custom-call(f32[128,128]{1,0:T(8,128)S(1)} %cholesky.115), custom_call_target="Cholesky" | custom-call | tf_op jit(solution)/shard_map/jit(cholesky)/cholesky | solution.py:55
  173.6 9.8 %custom-call.15 = f32[1,128,128]{1,2,0:T(8,128)S(1)} custom-call(f32[1,128,128]{2,1,0:T(8,128)S(1)} %get-tuple-element.29), custom_call_target="InvertDiagBlocksLowerTriangular" | custom-call | tf_op jit(solution)/shard_map/jit(cholesky)/cholesky | solution.py:55
  183.4 0.2 fusion.6
  183.7 0.3 convolution_subtract_fusion.2
  183.9 11.7 %cholesky.103 = f32[128,128]{1,0:T(8,128)S(1)} custom-call(f32[128,128]{1,0:T(8,128)S(1)} %convolution_subtract_fusion.2), custom_call_target="Cholesky" | custom-call | tf_op jit(solution)/shard_map/jit(cholesky)/cholesky | solution.py:55
  195.7 0.1 copy.16
  195.8 0.1 copy.15
  195.9 0.1 copy.14
  196.0 0.7 compare_reduce_fusion
  198.1 0.0 copy-start.1
  198.1 0.1 triangular_solve.60
  198.2 4.5 %while.1 = (s32[]{:T(128)}, f32[256,256]{0,1:T(8,128)S(1)}, s32[2,2]{1,0:T(2,128)S(1)}, f32[2,128,128]{2,1,0:T(8,128)S(1)}, s32[]{:T(128)}) while((s32[]{:T(128)}, f32[256,256]{0,1:T(8,128)S(1)}, s32[2,2]{1,0:T(2,128)S(1)}, f32[2,128,128]{2,1,0:T(8,128)S(1)}, s32[]{:T(128)}) %tuple.27), condition=%wide.while_cond, body=%wide.while_body.sunk | while | flops 2 | bytes 393321 | solution.py:26
  198.4 0.6 fusion.23
  199.0 1.4 dynamic-slice.7
  200.4 0.1 copy.23
  200.5 0.6 fusion.23
  201.1 1.4 dynamic-slice.7
  202.5 0.1 copy.23
  202.7 19.7 %custom-call.16 = f32[2,128,128]{1,2,0:T(8,128)S(1)} custom-call(f32[2,128,128]{2,1,0:T(8,128)S(1)} %get-tuple-element.9), custom_call_target="InvertDiagBlocksLowerTriangular" | custom-call | tf_op jit(solution)/shard_map/jit(_solve_triangular)/triangular_solve | solution.py:26
  222.4 3.0 reduce-scatter.4.cloned.1.call-done
  225.4 0.9 copy.20
  226.3 0.1 add_bitcast_fusion
  226.4 0.3 fusion.4
  226.7 0.3 convolution_subtract_fusion.1
  227.0 0.3 fusion.3
  227.3 0.1 fusion.8
  227.4 0.0 copy-start
  227.4 1.4 collective-permute-start
  228.8 5.6 %collective-permute-done = f32[64,256]{1,0:T(8,128)S(1)} collective-permute-done((f32[64,256]{1,0:T(8,128)S(1)}, f32[64,256]{1,0:T(8,128)S(1)}, u32[]{:S(2)}, u32[]{:S(2)}) %collective-permute-start) | collective-permute-done | bytes 65568 | tf_op jit(solution)/shard_map/ppermute | solution.py:60
  234.4 0.0 collective-permute-start.1
  234.4 7.0 %collective-permute-done.1 = f32[64,256]{1,0:T(8,128)S(1)} collective-permute-done((f32[64,256]{1,0:T(8,128)S(1)}, f32[64,256]{1,0:T(8,128)S(1)}, u32[]{:S(2)}, u32[]{:S(2)}) %collective-permute-start.1) | collective-permute-done | bytes 65568 | tf_op jit(solution)/shard_map/ppermute | solution.py:60
  241.4 0.0 collective-permute-start.2
  241.4 7.2 %collective-permute-done.2 = f32[64,256]{1,0:T(8,128)S(1)} collective-permute-done((f32[64,256]{1,0:T(8,128)S(1)}, f32[64,256]{1,0:T(8,128)S(1)}, u32[]{:S(2)}, u32[]{:S(2)}) %collective-permute-start.2) | collective-permute-done | bytes 65568 | tf_op jit(solution)/shard_map/ppermute | solution.py:60
  248.6 0.0 collective-permute-start.3
  248.6 7.0 %collective-permute-done.3 = f32[64,256]{1,0:T(8,128)S(1)} collective-permute-done((f32[64,256]{1,0:T(8,128)S(1)}, f32[64,256]{1,0:T(8,128)S(1)}, u32[]{:S(2)}, u32[]{:S(2)}) %collective-permute-start.3) | collective-permute-done | bytes 65568 | tf_op jit(solution)/shard_map/ppermute | solution.py:60
  255.5 0.0 collective-permute-start.4
  255.5 7.0 %collective-permute-done.4 = f32[64,256]{1,0:T(8,128)S(1)} collective-permute-done((f32[64,256]{1,0:T(8,128)S(1)}, f32[64,256]{1,0:T(8,128)S(1)}, u32[]{:S(2)}, u32[]{:S(2)}) %collective-permute-start.4) | collective-permute-done | bytes 65568 | tf_op jit(solution)/shard_map/ppermute | solution.py:60
  262.5 0.0 collective-permute-start.5
  262.5 7.0 %collective-permute-done.5 = f32[64,256]{1,0:T(8,128)S(1)} collective-permute-done((f32[64,256]{1,0:T(8,128)S(1)}, f32[64,256]{1,0:T(8,128)S(1)}, u32[]{:S(2)}, u32[]{:S(2)}) %collective-permute-start.5) | collective-permute-done | bytes 65568 | tf_op jit(solution)/shard_map/ppermute | solution.py:60
  269.5 0.0 collective-permute-start.6
  269.5 7.0 %collective-permute-done.6 = f32[64,256]{1,0:T(8,128)S(1)} collective-permute-done((f32[64,256]{1,0:T(8,128)S(1)}, f32[64,256]{1,0:T(8,128)S(1)}, u32[]{:S(2)}, u32[]{:S(2)}) %collective-permute-start.6) | collective-permute-done | bytes 65568 | tf_op jit(solution)/shard_map/ppermute | solution.py:60
  276.6 0.7 dynamic-slice_select_fusion.1
  277.3 0.0 all-reduce.9.cloned.1.call-update
  277.3 29.2 %all-reduce.9.cloned.1.call-done = f32[128,256]{1,0:T(8,128)} async-done(((f32[128,256]{1,0:T(8,128)}), f32[128,256]{1,0:T(8,128)}) %all-reduce.9.cloned.1.call-update) | async-done | bytes 131088 | tf_op jit(solution)/shard_map/psum | solution.py:11
  306.5 0.0 copy-done.1
  306.5 2.2 convolution_subtract_fusion
  308.7 0.0 copy-done
  (32 shorter events, 0.3 us)
Async XLA Ops:
  7.2 76.6 %all-reduce.5.cloned.1.call-start = ((), (), s32[]{:S(2)}) async-start(), calls=%async_computation.1 | async-start | bytes 6291456 | tf_op jit(solution)/shard_map/psum | solution.py:11
  12.4 147.2 %all-reduce.7.cloned.1.call-start = ((), (), s32[]{:S(2)}) async-start(), calls=%async_computation.2 | async-start | bytes 524288 | tf_op jit(solution)/shard_map/psum | solution.py:53
  88.3 137.1 %reduce-scatter.4.cloned.1.call-start = ((), (), s32[]{:S(2)}) async-start(), calls=%async_computation.4 | async-start | bytes 589824
  95.0 211.6 %all-reduce.9.cloned.1.call-start = ((), (), s32[]{:S(2)}) async-start(), calls=%async_computation.3 | async-start | bytes 262144 | tf_op jit(solution)/shard_map/psum | solution.py:11
  198.1 108.4 %copy-start.1 = (f32[512,128]{1,0:T(8,128)S(1)}, f32[512,128]{1,0:T(8,128)}, u32[]{:S(2)}) copy-start(f32[512,128]{1,0:T(8,128)} %param.5) | copy-start | bytes 786436
  227.4 81.3 %copy-start = (f32[64,256]{1,0:T(8,128)}, f32[64,256]{1,0:T(8,128)S(1)}, u32[]{:S(2)}) copy-start(f32[64,256]{1,0:T(8,128)S(1)} %fusion.8) | copy-start | bytes 196612
  227.4 7.0 %collective-permute-start = (f32[64,256]{1,0:T(8,128)S(1)}, f32[64,256]{1,0:T(8,128)S(1)}, u32[]{:S(2)}, u32[]{:S(2)}) collective-permute-start(f32[64,256]{1,0:T(8,128)S(1)} %fusion.8), channel_id=1, source_target_pairs={{0,1},{1,2},{2,3},{3,4},{4,5},{5,6},{6,7},{7,0},{8,9},{9,10},{10,1... | collective-permute-start | bytes 196616 | tf_op jit(solution)/shard_map/ppermute | solution.py:60
  234.4 7.0 %collective-permute-start.1 = (f32[64,256]{1,0:T(8,128)S(1)}, f32[64,256]{1,0:T(8,128)S(1)}, u32[]{:S(2)}, u32[]{:S(2)}) collective-permute-start(f32[64,256]{1,0:T(8,128)S(1)} %collective-permute-done), channel_id=1, source_target_pairs={{0,1},{1,2},{2,3},{3,4},{4,5},{5,6},{6,7},{7,0},{8,9},{9,10},{10,1... | collective-permute-start | bytes 196616 | tf_op jit(solution)/shard_map/ppermute | solution.py:60
  241.4 7.2 %collective-permute-start.2 = (f32[64,256]{1,0:T(8,128)S(1)}, f32[64,256]{1,0:T(8,128)S(1)}, u32[]{:S(2)}, u32[]{:S(2)}) collective-permute-start(f32[64,256]{1,0:T(8,128)S(1)} %collective-permute-done.1), channel_id=1, source_target_pairs={{0,1},{1,2},{2,3},{3,4},{4,5},{5,6},{6,7},{7,0},{8,9},{9,10},{10,1... | collective-permute-start | bytes 196616 | tf_op jit(solution)/shard_map/ppermute | solution.py:60
  248.6 7.0 %collective-permute-start.3 = (f32[64,256]{1,0:T(8,128)S(1)}, f32[64,256]{1,0:T(8,128)S(1)}, u32[]{:S(2)}, u32[]{:S(2)}) collective-permute-start(f32[64,256]{1,0:T(8,128)S(1)} %collective-permute-done.2), channel_id=1, source_target_pairs={{0,1},{1,2},{2,3},{3,4},{4,5},{5,6},{6,7},{7,0},{8,9},{9,10},{10,1... | collective-permute-start | bytes 196616 | tf_op jit(solution)/shard_map/ppermute | solution.py:60
  255.5 7.0 %collective-permute-start.4 = (f32[64,256]{1,0:T(8,128)S(1)}, f32[64,256]{1,0:T(8,128)S(1)}, u32[]{:S(2)}, u32[]{:S(2)}) collective-permute-start(f32[64,256]{1,0:T(8,128)S(1)} %collective-permute-done.3), channel_id=1, source_target_pairs={{0,1},{1,2},{2,3},{3,4},{4,5},{5,6},{6,7},{7,0},{8,9},{9,10},{10,1... | collective-permute-start | bytes 196616 | tf_op jit(solution)/shard_map/ppermute | solution.py:60
  262.5 7.0 %collective-permute-start.5 = (f32[64,256]{1,0:T(8,128)S(1)}, f32[64,256]{1,0:T(8,128)S(1)}, u32[]{:S(2)}, u32[]{:S(2)}) collective-permute-start(f32[64,256]{1,0:T(8,128)S(1)} %collective-permute-done.4), channel_id=1, source_target_pairs={{0,1},{1,2},{2,3},{3,4},{4,5},{5,6},{6,7},{7,0},{8,9},{9,10},{10,1... | collective-permute-start | bytes 196616 | tf_op jit(solution)/shard_map/ppermute | solution.py:60
  269.5 7.0 %collective-permute-start.6 = (f32[64,256]{1,0:T(8,128)S(1)}, f32[64,256]{1,0:T(8,128)S(1)}, u32[]{:S(2)}, u32[]{:S(2)}) collective-permute-start(f32[64,256]{1,0:T(8,128)S(1)} %collective-permute-done.5), channel_id=1, source_target_pairs={{0,1},{1,2},{2,3},{3,4},{4,5},{5,6},{6,7},{7,0},{8,9},{9,10},{10,1... | collective-permute-start | bytes 196616 | tf_op jit(solution)/shard_map/ppermute | solution.py:60
Sparse Core Ops, SparseCore 0:
  12.6 71.1 all-reduce.4
  88.4 71.1 all-reduce.6
  162.9 62.3 reduce-scatter.3
  277.5 28.9 all-reduce.8
